TPU v7x, 32 devices: a whole 2x2x4 slice. The times are simulated.
32 devices in a mesh: fsdp: 4 (over y, x), req: 8 (over z, core).
Axes of the slice: x: 2, y: 2, z: 4, core: 2. Of those that a mesh axis runs over, the one named last changes fastest.
Arguments:
- x_prompt: bfloat16 [8, 256, 2048], P('req', 'fsdp')
- x_suffix: bfloat16 [8, 4, 256, 2048], P('req', 'fsdp')
- norm_gain: float32 [2048], replicated, may hold values from 0.1 to 1.9
- w_query: bfloat16 [2048, 1024], P('fsdp', 'req')
- w_key: bfloat16 [2048, 512], P('fsdp', 'req')
- w_value: bfloat16 [2048, 512], P('fsdp', 'req'), may hold values from -0.125 to 0.125
- query_gain: float32 [128], replicated
- key_gain: float32 [128], replicated
- adapter_down: bfloat16 [8, 16, 2048], P('fsdp'), may hold values from -0.125 to 0.125
- adapter_up: bfloat16 [8, 16, 1024], P('fsdp'), may hold values from -1.5 to 1.5
- prompt_len: int32 [8], P('req'), may hold values from 64 to 256, as said below
- member_count: int32 [8], P('req'), may hold values from 2 to 4, as said below
- suffix_len: int32 [8, 4], P('req', 'fsdp'), may hold values from 128 to 256, as said below
- adapter_id: int32 [8, 4], P('req'), may hold values from 0 to 7
- holder_slot: int32 [8], replicated, may hold values from 0 to 7, each once
Outputs:
- prompt_out: bfloat16 [8, 256, 1024], P('req', 'fsdp')
- suffix_out: bfloat16 [8, 4, 256, 1024], P('req', 'fsdp')
Inputs may be any that keep to these rules, and one draw needn't show every extreme that they name: `prompt_len`: some group's prompt has exactly 256 positions. `member_count`: some group is full. `suffix_len`: some member's suffix has exactly 256 tokens. `holder_slot`: each adapter has its own storage row.
All inputs are finite; a program needn't handle non-finite values.
Results may differ from a plain program's by a relative error of at most 0.0055.
The roundings to bfloat16 on the way count: a program that leaves them out, or rounds other values in their place, can miss the bound.
Values may be sent and summed in bfloat16 or wider, within the bound.
No kernel may reach another device: no remote copies, remote signals or barrier semaphores. Data moves between devices by JAX's collectives and lax.ppermute only.
A program may use at most 64 MiB of HBM per device.

v0:
```python
import jax
import jax.numpy as jnp
from jax import lax
from jax.sharding import PartitionSpec as P

epsilon = 1e-06
rope_base = 1000000.0
masked_low = -1e30


def norm_rows(values, gain_vector):
    return (
        values
        * lax.rsqrt(jnp.mean(values * values, axis=-1, keepdims=True) + epsilon)
        * gain_vector
    )


def rotate(heads_in, positions):
    half_dim = heads_in.shape[-1] // 2
    frequency = rope_base ** (-jnp.arange(half_dim).astype(jnp.float32) / half_dim)
    angles = positions.astype(jnp.float32)[:, None] * frequency[None, :]
    cosine = jnp.cos(angles)[:, None, :]
    sine = jnp.sin(angles)[:, None, :]
    first_half = heads_in[..., :half_dim]
    second_half = heads_in[..., half_dim:]
    return jnp.concatenate(
        [first_half * cosine - second_half * sine, second_half * cosine + first_half * sine],
        axis=-1,
    )


def shape_heads(flat_rows, gain_vector, positions, head_dim):
    per_head = flat_rows.reshape(flat_rows.shape[0], flat_rows.shape[1] // head_dim, head_dim)
    return rotate(norm_rows(per_head, gain_vector), positions)


def update(carried, scores, allowed, value_heads, pattern):
    running, denominator, summed_output = carried
    masked = jnp.where(allowed, scores, masked_low)
    newest = jnp.maximum(running, jnp.max(masked, axis=-1))
    weights = jnp.where(allowed, jnp.exp(scores - newest[..., None]), 0.0)
    factor = jnp.exp(running - newest)
    denominator = denominator * factor + jnp.sum(weights, axis=-1)
    summed_output = summed_output * factor[..., None] + jnp.einsum(
        pattern, weights.astype(jnp.bfloat16), value_heads, preferred_element_type=jnp.float32
    )
    return (newest, denominator, summed_output)


def shards(
    x_prompt,
    x_suffix,
    norm_gain,
    w_query,
    w_key,
    w_value,
    query_gain,
    key_gain,
    adapter_down,
    adapter_up,
    prompt_len,
    member_count,
    suffix_len,
    adapter_id,
    holder_slot,
):
    fsdp_rank = lax.axis_index("fsdp")
    req_count = lax.axis_size("req")
    pr_rows = x_prompt.shape[1]
    mem_dev = x_suffix.shape[1]
    suf_rows = x_suffix.shape[2]
    model_width = x_prompt.shape[2]
    head_dim = query_gain.shape[0]
    q_cols = w_query.shape[1] * req_count
    kv_cols = w_key.shape[1] * req_count
    kv_heads = kv_cols // head_dim
    group_size = q_cols // kv_cols
    row_count = pr_rows + mem_dev * suf_rows
    prompt_total = prompt_len[0]
    tokens = jnp.concatenate(
        [x_prompt[0], x_suffix[0].reshape(mem_dev * suf_rows, model_width)], axis=0
    )
    normed = norm_rows(tokens.astype(jnp.float32), norm_gain).astype(jnp.bfloat16)
    full_q, full_k, full_v = (
        lax.all_gather(w_query, "req", axis=1, tiled=True),
        lax.all_gather(w_key, "req", axis=1, tiled=True),
        lax.all_gather(w_value, "req", axis=1, tiled=True),
    )
    pieces = (
        lax.all_gather(full_q, "fsdp", axis=0, tiled=True),
        lax.all_gather(full_k, "fsdp", axis=0, tiled=True),
        lax.all_gather(full_v, "fsdp", axis=0, tiled=True),
    )
    base_q, base_k, base_v = tuple(
        (
            jnp.dot(normed, weight_piece, preferred_element_type=jnp.float32)
            for weight_piece in pieces
        )
    )
    member_ids = adapter_id[0]
    store_rows = holder_slot.shape[0]
    lookup = jnp.where(
        member_ids[:, None] == jnp.arange(store_rows)[None, :], holder_slot[None, :], 0
    )
    storage = jnp.sum(lookup, axis=1)
    store_down, store_up = (
        lax.all_gather(adapter_down, "fsdp", axis=0, tiled=True),
        lax.all_gather(adapter_up, "fsdp", axis=0, tiled=True),
    )
    mine = lax.dynamic_slice_in_dim(storage, fsdp_rank * mem_dev, mem_dev)
    select_down_matrix = jnp.take(store_down, mine, axis=0)
    select_up_matrix = jnp.take(store_up, mine, axis=0)
    suffix_input_rows = normed[pr_rows:].reshape(mem_dev, suf_rows, model_width)
    reduced_rank_rows = jnp.einsum(
        "bve,bfe->bvf", suffix_input_rows, select_down_matrix, preferred_element_type=jnp.float32
    ).astype(jnp.bfloat16)
    adapter_delta = jnp.einsum(
        "wge,wet->wgt", reduced_rank_rows, select_up_matrix, preferred_element_type=jnp.float32
    )
    query_full = jnp.concatenate(
        [base_q[:pr_rows], base_q[pr_rows:] + adapter_delta.reshape(mem_dev * suf_rows, q_cols)],
        axis=0,
    )
    prompt_pos = fsdp_rank * pr_rows + jnp.arange(pr_rows)
    suffix_pos = prompt_total + jnp.tile(jnp.arange(suf_rows), mem_dev)
    positions = jnp.concatenate([prompt_pos, suffix_pos])
    queries = (
        shape_heads(query_full, query_gain, positions, head_dim)
        .astype(jnp.bfloat16)
        .reshape(row_count, kv_heads, group_size, head_dim)
    )
    key_heads = shape_heads(base_k, key_gain, positions, head_dim).astype(jnp.bfloat16)
    value_heads = base_v.astype(jnp.bfloat16).reshape(row_count, kv_heads, head_dim)
    limits = jnp.concatenate([prompt_pos, jnp.full((mem_dev * suf_rows,), 2**30, jnp.int32)])
    score_scale = head_dim ** (-0.5)
    start_state = (
        jnp.full((row_count, kv_heads, group_size), masked_low, jnp.float32),
        jnp.zeros((row_count, kv_heads, group_size), jnp.float32),
        jnp.zeros((row_count, kv_heads, group_size, head_dim), jnp.float32),
    )
    prompt_k_flat = key_heads[:pr_rows].reshape(pr_rows, kv_cols)
    prompt_v_flat = value_heads[:pr_rows].reshape(pr_rows, kv_cols)
    piece_keys = lax.all_gather(prompt_k_flat, "fsdp", axis=0, tiled=True)
    piece_values = lax.all_gather(prompt_v_flat, "fsdp", axis=0, tiled=True)
    piece_rows = piece_keys.shape[0]
    key_pos = jnp.arange(piece_rows)
    allowed = (key_pos[None, :] < prompt_total) & (key_pos[None, :] <= limits[:, None])
    scores = (
        jnp.einsum(
            "rkgd,nkd->rkgn",
            queries,
            piece_keys.reshape(piece_rows, kv_heads, head_dim),
            preferred_element_type=jnp.float32,
        )
        * score_scale
    )
    carried = update(
        start_state,
        scores,
        allowed[:, None, None, :],
        piece_values.reshape(piece_rows, kv_heads, head_dim),
        "rkgn,nkd->rkgd",
    )
    suffix_state = tuple(
        (
            state_part[pr_rows:].reshape((mem_dev, suf_rows) + state_part.shape[1:])
            for state_part in carried
        )
    )
    suffix_q = queries[pr_rows:].reshape(mem_dev, suf_rows, kv_heads, group_size, head_dim)
    suffix_k = key_heads[pr_rows:].reshape(mem_dev, suf_rows, kv_heads, head_dim)
    suffix_v = value_heads[pr_rows:].reshape(mem_dev, suf_rows, kv_heads, head_dim)
    own_scores = (
        jnp.einsum("mskgd,mtkd->mskgt", suffix_q, suffix_k, preferred_element_type=jnp.float32)
        * score_scale
    )
    causal = jnp.arange(suf_rows)[None, :] <= jnp.arange(suf_rows)[:, None]
    suffix_state = update(
        suffix_state, own_scores, causal[None, :, None, None, :], suffix_v, "mskgt,mtkd->mskgd"
    )
    denominator = jnp.concatenate(
        [carried[1][:pr_rows], suffix_state[1].reshape(mem_dev * suf_rows, kv_heads, group_size)],
        axis=0,
    )
    summed_output = jnp.concatenate(
        [
            carried[2][:pr_rows],
            suffix_state[2].reshape(mem_dev * suf_rows, kv_heads, group_size, head_dim),
        ],
        axis=0,
    )
    attended = (summed_output / denominator[..., None]).reshape(row_count, q_cols)
    member_index = fsdp_rank * mem_dev + jnp.arange(mem_dev)
    suffix_ok = (member_index < member_count[0])[:, None] & (
        jnp.arange(suf_rows)[None, :] < suffix_len[0][:, None]
    )
    valid_rows = jnp.concatenate([prompt_pos < prompt_total, suffix_ok.reshape(mem_dev * suf_rows)])
    result = jnp.where(valid_rows[:, None], attended, 0.0).astype(jnp.bfloat16)
    return (result[:pr_rows][None], result[pr_rows:].reshape(1, mem_dev, suf_rows, q_cols))


def solution(mesh):
    return jax.shard_map(
        shards,
        mesh=mesh,
        in_specs=(
            P("req", "fsdp", None),
            P("req", "fsdp", None, None),
            P(),
            P("fsdp", "req"),
            P("fsdp", "req"),
            P("fsdp", "req"),
            P(),
            P(),
            P("fsdp", None, None),
            P("fsdp", None, None),
            P("req"),
            P("req"),
            P("req", "fsdp"),
            P("req", None),
            P(),
        ),
        out_specs=(P("req", "fsdp", None), P("req", "fsdp", None, None)),
        check_vma=False,
    )
```

profile of v0, /device:TPU:0, one launch (start us, length us, event | category | flops | bytes accessed | tf_op | source)
XLA Modules:
  0.0 200.5 jit_solution(7296874157899483863)
XLA Ops:
  7.3 0.7 all-gather.7.cloned.1.call-update
  7.9 0.0 all-gather.11.cloned.1.call-start
  8.0 18.0 %all_gather.37 = bf16[512,512]{0,1:T(8,128)(2,1)} all-gather(bf16[512,64]{0,1:T(8,128)(2,1)} %param.20), channel_id=1, replica_groups=mesh['fsdp'=4,'req'=8] {'req'}, dimensions={1}, use_global_device_ids=true | all-gather | bytes 589824 | tf_op jit(solution)/shard_map/all_gather | solution.py:88
  26.0 0.0 all-gather.5.cloned.1.call-start
  26.1 17.6 %all_gather.30 = bf16[512,512]{0,1:T(8,128)(2,1)} all-gather(bf16[512,64]{0,1:T(8,128)(2,1)} %param.19), channel_id=1, replica_groups=mesh['fsdp'=4,'req'=8] {'req'}, dimensions={1}, use_global_device_ids=true | all-gather | bytes 589824 | tf_op jit(solution)/shard_map/all_gather | solution.py:87
  43.7 0.0 all-gather.9.cloned.1.call-start
  43.8 0.5 all-gather.9.cloned.1.call-update
  44.3 0.2 select_reduce_fusion
  44.5 0.6 dynamic_slice.3
  49.0 10.7 %all_gather.36 = bf16[8,16,1024]{2,1,0:T(8,128)(2,1)} all-gather(bf16[2,16,1024]{2,1,0:T(8,128)(2,1)S(1)} %copy-done.7), channel_id=1, replica_groups=mesh['fsdp'=4,'req'=8] {'fsdp'}, dimensions={0}, use_global_device_ids=true | all-gather | bytes 327680 | tf_op jit(solution)/shard_map/all_gather | solution.py:109
  59.7 0.4 fusion
  60.1 15.3 %all_gather.35 = bf16[8,16,2048]{2,1,0:T(8,128)(2,1)} all-gather(bf16[2,16,2048]{2,1,0:T(8,128)(2,1)S(1)} %copy-done.6), channel_id=1, replica_groups=mesh['fsdp'=4,'req'=8] {'fsdp'}, dimensions={0}, use_global_device_ids=true | all-gather | bytes 655360 | tf_op jit(solution)/shard_map/all_gather | solution.py:108
  75.5 0.1 pad_add_fusion
  75.6 0.1 fusion.63
  75.7 0.1 fusion.36
  75.8 0.6 multiply_cosine_fusion
  76.5 0.4 fusion.2
  76.9 2.0 %all-gather.11.cloned.1.call-done = bf16[2048,512]{0,1:T(8,128)(2,1)} async-done(((bf16[512,512]{0,1:T(8,128)(2,1)}), bf16[2048,512]{0,1:T(8,128)(2,1)}) %all-gather.11.cloned.1.call-update) | async-done | bytes 2097168 | tf_op jit(solution)/shard_map/all_gather | solution.py:93
  78.9 2.5 %convolution_convert_fusion = bf16[320,512]{1,0:T(8,128)(2,1)S(1)} fusion(bf16[320,2048]{1,0:T(8,128)(2,1)S(1)} %fusion.2, bf16[2048,512]{0,1:T(8,128)(2,1)} %all-gather.11.cloned.1.call-done), kind=kOutput, calls=%fused_computation.37 | convolution fusion | flops 671252480 | bytes 3735552 | tf_op jit(solution)/shard_map/dot_general | solution.py:97
  81.4 0.9 copy.124
  82.2 33.7 %all-gather.5.cloned.1.call-done = bf16[2048,512]{0,1:T(8,128)(2,1)} async-done(((bf16[512,512]{0,1:T(8,128)(2,1)}), bf16[2048,512]{0,1:T(8,128)(2,1)}) %all-gather.5.cloned.1.call-update) | async-done | bytes 2097168 | tf_op jit(solution)/shard_map/all_gather | solution.py:92
  115.9 2.5 %fusion.64 = f32[320,512]{1,0:T(8,128)S(1)} fusion(bf16[320,2048]{1,0:T(8,128)(2,1)S(1)} %fusion.2, bf16[2048,512]{0,1:T(8,128)(2,1)} %all-gather.5.cloned.1.call-done), kind=kOutput, calls=%fused_computation.109 | convolution fusion | flops 671088640 | bytes 4063232 | tf_op jit(solution)/shard_map/dot_general | solution.py:97
  118.4 0.2 reshape.286
  118.6 0.4 multiply_reduce_fusion.1
  119.1 0.1 copy.94
  119.2 0.2 fusion.31
  119.4 0.3 subtract_convert_fusion.1
  119.8 0.1 copy_bitcast_fusion
  119.8 10.2 %all_gather.32 = bf16[256,512]{1,0:T(8,128)(2,1)S(1)} all-gather(bf16[64,512]{1,0:T(8,128)(2,1)S(1)} %copy_bitcast_fusion), channel_id=1, replica_groups=mesh['fsdp'=4,'req'=8] {'fsdp'}, dimensions={0}, use_global_device_ids=true | all-gather | bytes 327680 | tf_op jit(solution)/shard_map/all_gather | solution.py:144
  130.1 0.9 copy.97
  130.9 10.5 %all_gather.39 = bf16[256,512]{1,0:T(8,128)(2,1)S(1)} all-gather(bf16[64,512]{1,0:T(8,128)(2,1)S(1)} %slice-done), channel_id=1, replica_groups=mesh['fsdp'=4,'req'=8] {'fsdp'}, dimensions={0}, use_global_device_ids=true | all-gather | bytes 327680 | tf_op jit(solution)/shard_map/all_gather | solution.py:145
  141.5 0.8 reshape.290
  142.2 30.4 %all-gather.9.cloned.1.call-done = bf16[2048,1024]{1,0:T(8,128)(2,1)} async-done(((bf16[512,1024]{1,0:T(8,128)(2,1)}), bf16[2048,1024]{1,0:T(8,128)(2,1)}) %all-gather.9.cloned.1.call-update) | async-done | bytes 4194320 | tf_op jit(solution)/shard_map/all_gather | solution.py:91
  172.6 4.8 %fusion.65 = f32[320,1024]{1,0:T(8,128)} fusion(bf16[320,2048]{1,0:T(8,128)(2,1)S(1)} %fusion.2, bf16[2048,1024]{1,0:T(8,128)(2,1)} %all-gather.9.cloned.1.call-done), kind=kOutput, calls=%fused_computation.110 | convolution fusion | flops 1342177280 | bytes 6815744 | tf_op jit(solution)/shard_map/dot_general | solution.py:97
  177.4 1.7 slice.99
  179.1 2.2 %convolution_add_fusion = f32[256,1024]{1,0:T(8,128)S(1)} fusion(bf16[320,2048]{1,0:T(8,128)(2,1)S(1)} %fusion.2, f32[320,1024]{1,0:T(8,128)} %fusion.65, bf16[8,16,2048]{2,1,0:T(8,128)(2,1)} %all_gather.35, s32[]{:T(128)} %bitcast.10, pred[]{:T(512)} %bitcast.9, bf16[8,16,1024]{2,1,0:T(8,128)(2,1)} %all_gather.36), kind=kOutput, calls=%fused_computation.25 | convolution fusion | flops 25481216 | bytes 3246080 | tf_op jit(solution)/shard_map/wge,wet->wgt/dot_general | solution.py:118
  181.3 1.1 maximum_bitcast_fusion
  182.4 0.3 copy.128
  182.7 0.4 multiply_reduce_fusion
  183.1 0.1 copy.98
  183.2 0.2 copy.99
  183.4 0.4 multiply_multiply_fusion
  183.8 0.6 subtract_convert_fusion
  184.4 0.1 copy.101
  184.5 0.3 pad_maximum_fusion.1
  184.8 0.1 copy.100
  184.9 0.1 copy.105
  185.0 0.5 copy-done.3
  185.4 1.0 fusion.3
  186.4 1.1 fusion.9
  187.6 0.6 fusion.6
  188.2 0.1 slice_maximum_fusion
  188.3 0.5 fusion.11
  188.7 0.1 fusion.51
  188.8 0.9 fusion.15
  189.7 0.0 copy-done.2
  189.8 1.0 fusion.21
  190.7 0.3 copy.109
  191.1 0.2 copy.123
  191.3 0.1 pad_maximum_fusion.3
  191.4 0.5 fusion.14
  191.9 0.2 slice_bitcast_fusion
  192.1 0.8 copy.111
  192.9 1.0 copy.112
  (46 shorter events, 0.3 us)
Async XLA Ops:
  7.2 37.1 %copy-start.11 = (s32[8]{0:T(128)S(1)}, s32[8]{0:T(128)}, u32[]{:S(2)}) copy-start(s32[8]{0:T(128)} %param.29) | copy-start | bytes 100
  7.2 37.1 %copy-start.12 = (s32[1,4]{1,0:T(1,128)S(1)}, s32[1,4]{1,0:T(1,128)}, u32[]{:S(2)}) copy-start(s32[1,4]{1,0:T(1,128)} %param.28) | copy-start | bytes 52
  7.2 41.8 %copy-start.7 = (bf16[2,16,1024]{2,1,0:T(8,128)(2,1)S(1)}, bf16[2,16,1024]{2,1,0:T(8,128)(2,1)}, u32[]{:S(2)}) copy-start(bf16[2,16,1024]{2,1,0:T(8,128)(2,1)} %param.24) | copy-start | bytes 196612
  7.2 52.5 %copy-start = (bf16[1,1,256,2048]{3,2,1,0:T(8,128)(2,1)S(1)}, bf16[1,1,256,2048]{3,2,1,0:T(8,128)(2,1)}, u32[]{:S(2)}) copy-start(bf16[1,1,256,2048]{3,2,1,0:T(8,128)(2,1)} %param.16) | copy-start | bytes 3145732
  7.2 52.5 %copy-start.1 = (bf16[1,64,2048]{2,1,0:T(8,128)(2,1)S(1)}, bf16[1,64,2048]{2,1,0:T(8,128)(2,1)}, u32[]{:S(2)}) copy-start(bf16[1,64,2048]{2,1,0:T(8,128)(2,1)} %param.15) | copy-start | bytes 786436
  7.2 36.6 %all-gather.7.cloned.1.call-start = ((), (), s32[]{:S(2)}) async-start(), calls=%async_computation.1 | async-start | bytes 1179648 | tf_op jit(solution)/shard_map/all_gather | solution.py:86
  7.9 70.9 %all-gather.11.cloned.1.call-start = ((), (), s32[]{:S(2)}) async-start(), calls=%async_computation.3 | async-start | bytes 2621440 | tf_op jit(solution)/shard_map/all_gather | solution.py:93
  26.0 34.1 %copy-start.6 = (bf16[2,16,2048]{2,1,0:T(8,128)(2,1)S(1)}, bf16[2,16,2048]{2,1,0:T(8,128)(2,1)}, u32[]{:S(2)}) copy-start(bf16[2,16,2048]{2,1,0:T(8,128)(2,1)} %param.23) | copy-start | bytes 393220
  26.0 89.9 %all-gather.5.cloned.1.call-start = ((), (), s32[]{:S(2)}) async-start(), calls=%async_computation | async-start | bytes 2621440 | tf_op jit(solution)/shard_map/all_gather | solution.py:92
  43.7 32.8 %copy-start.8 = (f32[2048]{0:T(1024)S(1)}, f32[2048]{0:T(1024)}, u32[]{:S(2)}) copy-start(f32[2048]{0:T(1024)} %param.17) | copy-start | bytes 24580
  43.7 128.9 %all-gather.9.cloned.1.call-start = ((), (), s32[]{:S(2)}) async-start(), calls=%async_computation.2 | async-start | bytes 5242880 | tf_op jit(solution)/shard_map/all_gather | solution.py:91
  81.4 0.9 copy-start.4
  118.4 0.8 copy-start.9
  119.4 11.5 %slice-start = ((bf16[320,512]{1,0:T(8,128)(2,1)}), bf16[64,512]{1,0:T(8,128)(2,1)S(1)}, s32[]{:S(2)}) async-start(bf16[320,512]{1,0:T(8,128)(2,1)} %copy-done.4), calls=%async_computation.4 | async-start | bytes 131072 | tf_op jit(solution)/shard_map/slice | solution.py:143
  182.4 1.0 copy-start.10
  184.5 1.0 copy-start.3
  187.6 1.2 copy-start.5
  188.8 1.0 copy-start.2
Sparse Core Ops, SparseCore 0:
  9.6 29.3 all-gather.6
  40.9 37.9 all-gather.10
  80.7 35.1 all-gather.4
  117.6 54.9 all-gather.8
where the time goes:
time: 201 us; the launch traced here: 200 us
  blocking collectives  82.4 us (41%)
  waiting for transfers between devices  67.3 us (33%)
  between operations  18.2 us (9%)
  matrix products  15.3 us (8%)
  local copies, waits for them, and re-layouts  8.99 us (4%)
  other arithmetic  8.1 us (4%)
    all_gather x1, waiting for transfers between devices, shards(): lax.all_gather(full_k, 'fsdp', axis=0, tiled=True)  33.7 us
    all_gather x1, waiting for transfers between devices, shards(): lax.all_gather(full_q, 'fsdp', axis=0, tiled=True)  30.4 us
    all_gather x1, blocking collectives, shards(): lax.all_gather(w_value, 'req', axis=1, tiled=True)  18 us
    all_gather x1, blocking collectives, shards(): lax.all_gather(w_key, 'req', axis=1, tiled=True)  17.6 us
    all_gather x1, blocking collectives, shards(): lax.all_gather(adapter_down, 'fsdp', axis=0, tiled=True)  15.3 us
    all_gather x1, blocking collectives, shards(): lax.all_gather(adapter_up, 'fsdp', axis=0, tiled=True)  10.7 us
    all_gather x1, blocking collectives, shards(): piece_values = lax.all_gather(prompt_v_flat, 'fsdp', axis=0, tiled=True)  10.5 us
    all_gather x1, blocking collectives, shards(): piece_keys = lax.all_gather(prompt_k_flat, 'fsdp', axis=0, tiled=True)  10.2 us
  transfers between devices with their start and end apart: 4, of which 3 were waited for; matrix products, arithmetic and copies ran while one was open for 6% of the time, Pallas kernels for 0%

commit v1 on v0

--- a/solution.py
+++ b/solution.py
@@ -141,8 +141,13 @@
     )
     prompt_k_flat = key_heads[:pr_rows].reshape(pr_rows, kv_cols)
     prompt_v_flat = value_heads[:pr_rows].reshape(pr_rows, kv_cols)
-    piece_keys = lax.all_gather(prompt_k_flat, "fsdp", axis=0, tiled=True)
-    piece_values = lax.all_gather(prompt_v_flat, "fsdp", axis=0, tiled=True)
+    piece_keys, piece_values = jnp.split(
+        lax.all_gather(
+            jnp.concatenate([prompt_k_flat, prompt_v_flat], axis=1), "fsdp", axis=0, tiled=True
+        ),
+        [prompt_k_flat.shape[1]],
+        axis=1,
+    )
     piece_rows = piece_keys.shape[0]
     key_pos = jnp.arange(piece_rows)
     allowed = (key_pos[None, :] < prompt_total) & (key_pos[None, :] <= limits[:, None])

time: 201 us -> 200 us (level)
  blocking collectives: 82.4 us -> 74.5 us
  local copies, waits for them, and re-layouts: 8.99 us -> 12.5 us
  waiting for transfers between devices: 67.3 us -> 70.8 us
    all_gather x2 -> x1, blocking collectives: 20.7 us -> 12.8 us  [shards(): lax.all_gather(jnp.concatenate([prompt_k_flat, prompt_v_flat], axis=1), '...]
    all_gather x1, waiting for transfers between devices: 30.4 us -> 33.7 us  [shards(): lax.all_gather(full_q, 'fsdp', axis=0, tiled=True)]
  transfers between devices with their start and end apart: 4 -> 4, of which waited for: 3 -> 3; matrix products, arithmetic and copies ran while one was open for 6% -> 7% of each run, Pallas kernels for 0% -> 0%
where the time goes in v1:
time: 200 us
  blocking collectives  74.5 us (37%)
  waiting for transfers between devices  70.8 us (35%)
  between operations  18.2 us (9%)
  matrix products  15.4 us (8%)
  local copies, waits for them, and re-layouts  12.5 us (6%)
  other arithmetic  8.11 us (4%)
    all_gather x1, waiting for transfers between devices, shards(): lax.all_gather(full_k, 'fsdp', axis=0, tiled=True)  33.8 us
    all_gather x1, waiting for transfers between devices, shards(): lax.all_gather(full_q, 'fsdp', axis=0, tiled=True)  33.7 us
    all_gather x1, blocking collectives, shards(): lax.all_gather(w_value, 'req', axis=1, tiled=True)  18 us
    all_gather x1, blocking collectives, shards(): lax.all_gather(w_key, 'req', axis=1, tiled=True)  17.6 us
    all_gather x1, blocking collectives, shards(): lax.all_gather(adapter_down, 'fsdp', axis=0, tiled=True)  15.4 us
    all_gather x1, blocking collectives, shards(): lax.all_gather(jnp.concatenate([prompt_k_flat, prompt_v_flat], axis=1), '...  12.8 us
    all_gather x1, blocking collectives, shards(): lax.all_gather(adapter_up, 'fsdp', axis=0, tiled=True)  10.7 us
    dot_general x3, matrix products, shards(): jnp.dot(normed, weight_piece, preferred_element_type=jnp.float32)  9.71 us
  transfers between devices with their start and end apart: 4, of which 3 were waited for; matrix products, arithmetic and copies ran while one was open for 7% of the time, Pallas kernels for 0%

profile of v1, /device:TPU:0, one launch (start us, length us, event | category | flops | bytes accessed | tf_op | source)
XLA Modules:
  0.0 199.7 jit_solution(6181205710699650206)
XLA Ops:
  7.3 0.7 all-gather.9.cloned.1.call-update
  8.0 18.0 %all_gather.29 = bf16[512,512]{0,1:T(8,128)(2,1)} all-gather(bf16[512,64]{0,1:T(8,128)(2,1)} %param.20), channel_id=1, replica_groups=mesh['fsdp'=4,'req'=8] {'req'}, dimensions={1}, use_global_device_ids=true | all-gather | bytes 589824 | tf_op jit(solution)/shard_map/all_gather | solution.py:88
  26.0 0.0 all-gather.5.cloned.1.call-start
  26.1 17.6 %all_gather.27 = bf16[512,512]{0,1:T(8,128)(2,1)} all-gather(bf16[512,64]{0,1:T(8,128)(2,1)} %param.19), channel_id=1, replica_groups=mesh['fsdp'=4,'req'=8] {'req'}, dimensions={1}, use_global_device_ids=true | all-gather | bytes 589824 | tf_op jit(solution)/shard_map/all_gather | solution.py:87
  43.8 0.5 all-gather.11.cloned.1.call-update
  44.3 0.2 select_reduce_fusion
  44.5 0.6 dynamic_slice.3
  49.0 10.7 %all_gather.35 = bf16[8,16,1024]{2,1,0:T(8,128)(2,1)} all-gather(bf16[2,16,1024]{2,1,0:T(8,128)(2,1)S(1)} %copy-done.7), channel_id=1, replica_groups=mesh['fsdp'=4,'req'=8] {'fsdp'}, dimensions={0}, use_global_device_ids=true | all-gather | bytes 327680 | tf_op jit(solution)/shard_map/all_gather | solution.py:109
  59.7 0.4 fusion
  60.1 15.4 %all_gather.34 = bf16[8,16,2048]{2,1,0:T(8,128)(2,1)} all-gather(bf16[2,16,2048]{2,1,0:T(8,128)(2,1)S(1)} %copy-done.6), channel_id=1, replica_groups=mesh['fsdp'=4,'req'=8] {'fsdp'}, dimensions={0}, use_global_device_ids=true | all-gather | bytes 655360 | tf_op jit(solution)/shard_map/all_gather | solution.py:108
  75.5 0.1 pad_add_fusion
  75.6 0.1 fusion.65
  75.7 0.1 fusion.36
  75.8 0.6 multiply_cosine_fusion
  76.5 0.4 fusion.2
  76.9 2.0 %all-gather.7.cloned.1.call-done = bf16[2048,512]{0,1:T(8,128)(2,1)} async-done(((bf16[512,512]{0,1:T(8,128)(2,1)}), bf16[2048,512]{0,1:T(8,128)(2,1)}) %all-gather.7.cloned.1.call-update) | async-done | bytes 2097168 | tf_op jit(solution)/shard_map/all_gather | solution.py:93
  78.9 2.5 %convolution_convert_fusion = bf16[320,512]{1,0:T(8,128)(2,1)S(1)} fusion(bf16[320,2048]{1,0:T(8,128)(2,1)S(1)} %fusion.2, bf16[2048,512]{0,1:T(8,128)(2,1)} %all-gather.7.cloned.1.call-done), kind=kOutput, calls=%fused_computation.37 | convolution fusion | flops 671252480 | bytes 3735552 | tf_op jit(solution)/shard_map/dot_general | solution.py:97
  81.4 0.7 copy-done.4
  82.1 33.8 %all-gather.5.cloned.1.call-done = bf16[2048,512]{0,1:T(8,128)(2,1)} async-done(((bf16[512,512]{0,1:T(8,128)(2,1)}), bf16[2048,512]{0,1:T(8,128)(2,1)}) %all-gather.5.cloned.1.call-update) | async-done | bytes 2097168 | tf_op jit(solution)/shard_map/all_gather | solution.py:92
  115.9 2.5 %fusion.66 = f32[320,512]{1,0:T(8,128)S(1)} fusion(bf16[320,2048]{1,0:T(8,128)(2,1)S(1)} %fusion.2, bf16[2048,512]{0,1:T(8,128)(2,1)} %all-gather.5.cloned.1.call-done), kind=kOutput, calls=%fused_computation.112 | convolution fusion | flops 671088640 | bytes 4063232 | tf_op jit(solution)/shard_map/dot_general | solution.py:97
  118.4 0.2 reshape.286
  118.6 0.4 multiply_reduce_fusion.1
  119.1 0.1 copy.92
  119.2 0.2 fusion.31
  119.4 0.3 subtract_convert_fusion.1
  119.8 0.1 copy_bitcast_fusion
  119.9 0.2 slice-done
  120.0 12.8 %all_gather.31 = bf16[256,1024]{1,0:T(8,128)(2,1)S(1)} all-gather(bf16[64,1024]{1,0:T(8,128)(2,1)S(1)} %pad_maximum_fusion.3), channel_id=1, replica_groups=mesh['fsdp'=4,'req'=8] {'fsdp'}, dimensions={0}, use_global_device_ids=true | all-gather | bytes 655360 | tf_op jit(solution)/shard_map/all_gather | solution.py:145
  132.9 0.9 fusion.64
  133.7 1.7 reshape.288
  135.5 1.7 reshape.290
  137.2 0.8 copy.121
  138.0 33.7 %all-gather.11.cloned.1.call-done = bf16[2048,1024]{1,0:T(8,128)(2,1)} async-done(((bf16[512,1024]{1,0:T(8,128)(2,1)}), bf16[2048,1024]{1,0:T(8,128)(2,1)}) %all-gather.11.cloned.1.call-update) | async-done | bytes 4194320 | tf_op jit(solution)/shard_map/all_gather | solution.py:91
  171.8 4.8 %fusion.67 = f32[320,1024]{1,0:T(8,128)} fusion(bf16[320,2048]{1,0:T(8,128)(2,1)S(1)} %fusion.2, bf16[2048,1024]{1,0:T(8,128)(2,1)} %all-gather.11.cloned.1.call-done), kind=kOutput, calls=%fused_computation.113 | convolution fusion | flops 1342177280 | bytes 6815744 | tf_op jit(solution)/shard_map/dot_general | solution.py:97
  176.6 1.7 slice.100
  178.2 2.2 %convolution_add_fusion = f32[256,1024]{1,0:T(8,128)S(1)} fusion(bf16[320,2048]{1,0:T(8,128)(2,1)S(1)} %fusion.2, f32[320,1024]{1,0:T(8,128)} %fusion.67, bf16[8,16,2048]{2,1,0:T(8,128)(2,1)} %all_gather.34, s32[]{:T(128)} %bitcast.9, pred[]{:T(512)} %bitcast.8, bf16[8,16,1024]{2,1,0:T(8,128)(2,1)} %all_gather.35), kind=kOutput, calls=%fused_computation.25 | convolution fusion | flops 25481216 | bytes 3246080 | tf_op jit(solution)/shard_map/wge,wet->wgt/dot_general | solution.py:118
  180.5 1.1 maximum_bitcast_fusion
  181.6 0.3 copy.125
  181.9 0.4 multiply_reduce_fusion
  182.3 0.1 copy.95
  182.4 0.2 copy.96
  182.6 0.4 multiply_multiply_fusion
  183.0 0.6 subtract_convert_fusion
  183.6 0.1 copy.97
  183.7 0.1 copy.98
  183.8 0.3 pad_maximum_fusion.1
  184.1 0.5 copy-done.3
  184.5 1.0 fusion.3
  185.6 0.1 copy.102
  185.6 0.6 fusion.6
  186.2 0.1 slice_maximum_fusion
  186.3 1.1 fusion.9
  187.5 0.5 fusion.11
  188.0 0.1 fusion.52
  188.1 0.9 fusion.15
  189.0 0.0 copy-done.2
  189.0 1.0 fusion.21
  190.0 0.3 copy.106
  190.3 0.2 copy.120
  190.5 0.1 pad_maximum_fusion.4
  190.6 0.5 fusion.14
  191.1 0.2 slice_bitcast_fusion
  191.4 1.0 copy.109
  192.4 0.8 copy.108
  (48 shorter events, 0.4 us)
Async XLA Ops:
  7.2 37.1 %copy-start.12 = (s32[1,4]{1,0:T(1,128)S(1)}, s32[1,4]{1,0:T(1,128)}, u32[]{:S(2)}) copy-start(s32[1,4]{1,0:T(1,128)} %param.28) | copy-start | bytes 52
  7.2 37.1 %copy-start.11 = (s32[8]{0:T(128)S(1)}, s32[8]{0:T(128)}, u32[]{:S(2)}) copy-start(s32[8]{0:T(128)} %param.29) | copy-start | bytes 100
  7.2 41.8 %copy-start.7 = (bf16[2,16,1024]{2,1,0:T(8,128)(2,1)S(1)}, bf16[2,16,1024]{2,1,0:T(8,128)(2,1)}, u32[]{:S(2)}) copy-start(bf16[2,16,1024]{2,1,0:T(8,128)(2,1)} %param.24) | copy-start | bytes 196612
  7.2 52.5 %copy-start.1 = (bf16[1,64,2048]{2,1,0:T(8,128)(2,1)S(1)}, bf16[1,64,2048]{2,1,0:T(8,128)(2,1)}, u32[]{:S(2)}) copy-start(bf16[1,64,2048]{2,1,0:T(8,128)(2,1)} %param.15) | copy-start | bytes 786436
  7.2 52.5 %copy-start = (bf16[1,1,256,2048]{3,2,1,0:T(8,128)(2,1)S(1)}, bf16[1,1,256,2048]{3,2,1,0:T(8,128)(2,1)}, u32[]{:S(2)}) copy-start(bf16[1,1,256,2048]{3,2,1,0:T(8,128)(2,1)} %param.16) | copy-start | bytes 3145732
  7.2 36.6 %all-gather.9.cloned.1.call-start = ((), (), s32[]{:S(2)}) async-start(), calls=%async_computation.2 | async-start | bytes 1179648 | tf_op jit(solution)/shard_map/all_gather | solution.py:86
  8.0 70.9 %all-gather.7.cloned.1.call-start = ((), (), s32[]{:S(2)}) async-start(), calls=%async_computation.1 | async-start | bytes 2621440 | tf_op jit(solution)/shard_map/all_gather | solution.py:93
  26.0 34.1 %copy-start.6 = (bf16[2,16,2048]{2,1,0:T(8,128)(2,1)S(1)}, bf16[2,16,2048]{2,1,0:T(8,128)(2,1)}, u32[]{:S(2)}) copy-start(bf16[2,16,2048]{2,1,0:T(8,128)(2,1)} %param.23) | copy-start | bytes 393220
  26.0 89.9 %all-gather.5.cloned.1.call-start = ((), (), s32[]{:S(2)}) async-start(), calls=%async_computation | async-start | bytes 2621440 | tf_op jit(solution)/shard_map/all_gather | solution.py:92
  43.7 32.8 %copy-start.8 = (f32[2048]{0:T(1024)S(1)}, f32[2048]{0:T(1024)}, u32[]{:S(2)}) copy-start(f32[2048]{0:T(1024)} %param.17) | copy-start | bytes 24580
  43.7 128.0 %all-gather.11.cloned.1.call-start = ((), (), s32[]{:S(2)}) async-start(), calls=%async_computation.3 | async-start | bytes 5242880 | tf_op jit(solution)/shard_map/all_gather | solution.py:91
  81.4 0.7 copy-start.4
  118.4 0.8 copy-start.9
  119.2 0.8 slice-start
  119.7 17.5 %slice-start.1 = ((bf16[320,512]{1,0:T(8,128)(2,1)}), bf16[256,512]{1,0:T(8,128)(2,1)S(1)}, s32[]{:S(2)}) async-start(bf16[320,512]{1,0:T(8,128)(2,1)} %copy-done.4), calls=%async_computation.5 | async-start | bytes 524288 | tf_op jit(solution)/shard_map/slice | solution.py:178
  181.6 1.0 copy-start.10
  183.6 1.0 copy-start.3
  186.3 1.7 copy-start.5
  188.1 1.0 copy-start.2
Sparse Core Ops, SparseCore 0:
  9.6 29.3 all-gather.8
  40.9 37.9 all-gather.6
  80.7 35.1 all-gather.4
  117.6 54.0 all-gather.10
